TPU v7x, 128 devices: a whole 4x4x4 slice. The times are simulated.
128 devices in a mesh: ctx: 64 (over z_lo, x, y, core), fsdp: 2 (over z_hi).
Axes of the slice: x: 4, y: 4, z: 4 (z_hi: 2, z_lo: 2; z = z_hi * 2 + z_lo), core: 2. Of those that a mesh axis runs over, the one named last changes fastest.
Arguments:
- block_in: bfloat16 [2, 8192, 768], P('fsdp', 'ctx'), may hold values from -70 to 70
- out_grad: bfloat16 [2, 8192, 768], P('fsdp', 'ctx'), may hold values from -6 to 6
- ln1_gain: bfloat16 [768], P('fsdp'), may hold values from 0.5 to 1.5
- ln1_bias: bfloat16 [768], P('fsdp'), may hold values from -3 to 3
- w_qkv: bfloat16 [768, 2304], P('fsdp'), may hold values from -2 to 2
- q_bias: bfloat16 [768], P('fsdp'), may hold values from -3 to 3
- v_bias: bfloat16 [768], P('fsdp'), may hold values from -3 to 3
- w_proj: bfloat16 [768, 768], P('fsdp'), may hold values from -2 to 2
- b_proj: bfloat16 [768], P('fsdp'), may hold values from -3 to 3
- ln2_gain: bfloat16 [768], P('fsdp'), may hold values from 0.5 to 1.5
- ln2_bias: bfloat16 [768], P('fsdp'), may hold values from -3 to 3
- w_fc: bfloat16 [768, 3072], P('fsdp'), may hold values from -0.21875 to 0.21875
- b_fc: bfloat16 [3072], P('fsdp'), may hold values from -3 to 3
- w_out: bfloat16 [3072, 768], P('fsdp'), may hold values from -0.109375 to 0.109375
- b_out: bfloat16 [768], P('fsdp'), may hold values from -3 to 3
Outputs:
- block_out: bfloat16 [2, 8192, 768], P('fsdp', 'ctx')
- input_grad: float32 [2, 8192, 768], P('fsdp', 'ctx')
- grad_ln1_gain: float32 [768], P('fsdp')
- grad_ln1_bias: float32 [768], P('fsdp')
- grad_w_qkv: float32 [768, 2304], P('fsdp')
- grad_q_bias: float32 [768], P('fsdp')
- grad_v_bias: float32 [768], P('fsdp')
- grad_w_proj: float32 [768, 768], P('fsdp')
- grad_b_proj: float32 [768], P('fsdp')
- grad_ln2_gain: float32 [768], P('fsdp')
- grad_ln2_bias: float32 [768], P('fsdp')
- grad_w_fc: float32 [768, 3072], P('fsdp')
- grad_b_fc: float32 [3072], P('fsdp')
- grad_w_out: float32 [3072, 768], P('fsdp')
- grad_b_out: float32 [768], P('fsdp')
All inputs are finite; a program needn't handle non-finite values.
Results may differ from a plain program's by a relative error of at most 0.025.
The roundings to bfloat16 on the way count: a program that leaves them out, or rounds other values in their place, can miss the bound.
Values may be sent and summed in bfloat16 or wider, within the bound.
No kernel may reach another device: no remote copies, remote signals or barrier semaphores. Data moves between devices by JAX's collectives and lax.ppermute only.
A program may use at most 256 MiB of HBM per device.

v0:
```python
import math
import jax
import jax.numpy as jnp
from jax import lax
from jax.sharding import PartitionSpec as P

HEADS = 12
norm_epsilon = 1e-05
gelu_factor = 0.7978845608028654
gelu_cubic = 0.044715
masked_score = -1e30


def layer_norm(values, gain, offset):
    center = jnp.mean(values, axis=-1, keepdims=True)
    centered = values - center
    spread = jnp.mean(centered * centered, axis=-1, keepdims=True)
    return centered * lax.rsqrt(spread + norm_epsilon) * gain + offset


def gelu_tanh(values):
    return (
        0.5
        * values
        * (1.0 + jnp.tanh(gelu_factor * (values + gelu_cubic * values * values * values)))
    )


def score_grads(
    query_rows, grad_rows, lse_rows, delta_rows, key_rows, value_rows, allowed, score_scale
):
    scores = (
        jnp.einsum("thd,shd->hts", query_rows, key_rows, preferred_element_type=jnp.float32)
        * score_scale
    )
    scores = jnp.where(allowed[None], scores, masked_score)
    probabilities = jnp.where(allowed[None], jnp.exp(scores - lse_rows[:, :, None]), 0.0)
    grad_probs = jnp.einsum(
        "thd,shd->hts", grad_rows, value_rows, preferred_element_type=jnp.float32
    )
    grad_scores = (probabilities * (grad_probs - delta_rows[:, :, None]) * score_scale).astype(
        jnp.bfloat16
    )
    return (grad_scores, probabilities)


def body(
    block_in,
    out_grad,
    ln1_gain,
    ln1_bias,
    w_qkv,
    q_bias,
    v_bias,
    w_proj,
    b_proj,
    ln2_gain,
    ln2_bias,
    w_fc,
    b_fc,
    w_out,
    b_out,
):
    gathered = (
        lax.all_gather(ln1_gain, "fsdp", axis=0, tiled=True),
        lax.all_gather(ln1_bias, "fsdp", axis=0, tiled=True),
        lax.all_gather(w_qkv, "fsdp", axis=0, tiled=True),
        lax.all_gather(q_bias, "fsdp", axis=0, tiled=True),
        lax.all_gather(v_bias, "fsdp", axis=0, tiled=True),
        lax.all_gather(w_proj, "fsdp", axis=0, tiled=True),
        lax.all_gather(b_proj, "fsdp", axis=0, tiled=True),
        lax.all_gather(ln2_gain, "fsdp", axis=0, tiled=True),
        lax.all_gather(ln2_bias, "fsdp", axis=0, tiled=True),
        lax.all_gather(w_fc, "fsdp", axis=0, tiled=True),
        lax.all_gather(b_fc, "fsdp", axis=0, tiled=True),
        lax.all_gather(w_out, "fsdp", axis=0, tiled=True),
        lax.all_gather(b_out, "fsdp", axis=0, tiled=True),
    )
    gain_one = gathered[0].astype(jnp.float32)
    shift_one = gathered[1].astype(jnp.float32)
    qkv_weight = gathered[2]
    query_bias = gathered[3].astype(jnp.float32)
    value_bias = gathered[4].astype(jnp.float32)
    proj_weight = gathered[5]
    proj_bias = gathered[6].astype(jnp.float32)
    gain_two = gathered[7].astype(jnp.float32)
    shift_two = gathered[8].astype(jnp.float32)
    fc_weight = gathered[9]
    fc_bias = gathered[10].astype(jnp.float32)
    out_weight = gathered[11]
    out_bias = gathered[12].astype(jnp.float32)
    row_count = block_in.shape[1]
    width = block_in.shape[2]
    head_count = HEADS
    head_width = width // head_count
    score_scale = 1.0 / math.sqrt(head_width)
    row_total = row_count * lax.axis_size("ctx")
    first_query = lax.axis_index("ctx") * row_count
    query_pos = first_query + jnp.arange(row_count, dtype=jnp.int32)
    last_query = first_query + row_count - 1
    inputs_wide = block_in[0].astype(jnp.float32)
    normed_one = layer_norm(inputs_wide, gain_one, shift_one).astype(jnp.bfloat16)
    projected = jnp.dot(normed_one, qkv_weight, preferred_element_type=jnp.float32)
    queries = (projected[:, :width] + query_bias).astype(jnp.bfloat16)
    keys_local = projected[:, width : 2 * width].astype(jnp.bfloat16)
    values_local = (projected[:, 2 * width :] + value_bias).astype(jnp.bfloat16)
    query_heads = queries.reshape(row_count, head_count, head_width)
    initial = (
        jnp.full((head_count, row_count), masked_score, jnp.float32),
        jnp.zeros((head_count, row_count), jnp.float32),
        jnp.zeros((row_count, head_count, head_width), jnp.float32),
    )
    key_span = lax.all_gather(keys_local, "ctx", axis=0, tiled=True)
    value_span = lax.all_gather(values_local, "ctx", axis=0, tiled=True)
    span_total = key_span.shape[0]
    attend_span_rows = math.gcd(span_total, 512)

    def one_step(step_index, inner):
        offset = step_index * attend_span_rows
        key_rows = lax.dynamic_slice_in_dim(key_span, offset, attend_span_rows, 0).reshape(
            attend_span_rows, head_count, head_width
        )
        value_rows = lax.dynamic_slice_in_dim(value_span, offset, attend_span_rows, 0).reshape(
            attend_span_rows, head_count, head_width
        )

        def one_computed(state):
            maximum, denominator, accumulated = state
            key_pos = offset + jnp.arange(attend_span_rows, dtype=jnp.int32)
            allowed = key_pos[None, :] <= query_pos[:, None]
            scores = (
                jnp.einsum(
                    "thd,shd->hts", query_heads, key_rows, preferred_element_type=jnp.float32
                )
                * score_scale
            )
            scores = jnp.where(allowed[None], scores, masked_score)
            new_max = jnp.maximum(maximum, jnp.max(scores, axis=2))
            weights = jnp.where(allowed[None], jnp.exp(scores - new_max[:, :, None]), 0.0)
            factor = jnp.exp(maximum - new_max)
            denominator = denominator * factor + jnp.sum(weights, axis=2)
            accumulated = accumulated * jnp.transpose(factor)[:, :, None] + jnp.einsum(
                "hts,shd->thd",
                weights.astype(jnp.bfloat16),
                value_rows,
                preferred_element_type=jnp.float32,
            )
            return (new_max, denominator, accumulated)

        return lax.cond(offset > last_query, lambda state: state, one_computed, inner)

    maximum, denominator, accumulated = lax.fori_loop(
        0, span_total // attend_span_rows, one_step, initial
    )
    log_sums = maximum + jnp.log(denominator)
    attended = accumulated / jnp.transpose(denominator)[:, :, None]
    attn_rows = lax.optimization_barrier(attended.reshape(row_count, width).astype(jnp.bfloat16))
    residual_one = (
        jnp.dot(attn_rows, proj_weight, preferred_element_type=jnp.float32)
        + proj_bias
        + inputs_wide
    )
    normed_two = layer_norm(residual_one, gain_two, shift_two).astype(jnp.bfloat16)
    hidden_pre = jnp.dot(normed_two, fc_weight, preferred_element_type=jnp.float32) + fc_bias
    activated = gelu_tanh(hidden_pre).astype(jnp.bfloat16)
    output = (
        jnp.dot(activated, out_weight, preferred_element_type=jnp.float32) + out_bias + residual_one
    ).astype(jnp.bfloat16)
    cotangent = out_grad[0]
    grad_wide = cotangent.astype(jnp.float32)
    grad_out_weight = jnp.einsum(
        "tf,td->fd", activated, cotangent, preferred_element_type=jnp.float32
    )
    grad_out_bias = jnp.sum(grad_wide, axis=0)
    grad_activated = jnp.einsum(
        "td,fd->tf", cotangent, out_weight, preferred_element_type=jnp.float32
    )
    unused, gelu_back = jax.vjp(gelu_tanh, hidden_pre)
    grad_hidden = gelu_back(grad_activated)[0]
    grad_hidden_low = grad_hidden.astype(jnp.bfloat16)
    grad_fc_weight = jnp.einsum(
        "td,tf->df", normed_two, grad_hidden_low, preferred_element_type=jnp.float32
    )
    grad_fc_bias = jnp.sum(grad_hidden, axis=0)
    grad_normed_two = jnp.einsum(
        "tf,df->td", grad_hidden_low, fc_weight, preferred_element_type=jnp.float32
    )
    unused, norm_back_two = jax.vjp(layer_norm, residual_one, gain_two, shift_two)
    grad_residual, grad_gain_two, grad_shift_two = norm_back_two(grad_normed_two)
    grad_residual = grad_residual + grad_wide
    grad_residual_low = grad_residual.astype(jnp.bfloat16)
    grad_proj_weight = jnp.einsum(
        "td,te->de", attn_rows, grad_residual_low, preferred_element_type=jnp.float32
    )
    grad_proj_bias = jnp.sum(grad_residual, axis=0)
    grad_attn = lax.optimization_barrier(
        jnp.einsum(
            "te,de->td", grad_residual_low, proj_weight, preferred_element_type=jnp.float32
        ).astype(jnp.bfloat16)
    )
    grad_heads = grad_attn.reshape(row_count, head_count, head_width)
    delta_sums = jnp.transpose(
        jnp.sum(
            grad_heads.astype(jnp.float32)
            * attn_rows.reshape(row_count, head_count, head_width).astype(jnp.float32),
            axis=2,
        )
    )
    keys_all, values_all = (
        lax.all_gather(keys_local, "ctx", axis=0, tiled=True),
        lax.all_gather(values_local, "ctx", axis=0, tiled=True),
    )
    span_rows = math.gcd(row_total, 512)
    span_count = row_total // span_rows
    key_blocks = keys_all.reshape(span_count, span_rows, head_count, head_width)
    value_blocks = values_all.reshape(span_count, span_rows, head_count, head_width)
    zero_query = jnp.zeros((row_count, head_count, head_width), jnp.float32)

    def back_step(grad_query, inputs):
        key_rows, value_rows, step_index = inputs
        start_pos = step_index * span_rows

        def back_computed(running):
            key_pos = start_pos + jnp.arange(span_rows, dtype=jnp.int32)
            allowed = key_pos[None, :] <= query_pos[:, None]
            grad_scores, probabilities = score_grads(
                query_heads,
                grad_heads,
                log_sums,
                delta_sums,
                key_rows,
                value_rows,
                allowed,
                score_scale,
            )
            rounded = probabilities.astype(jnp.bfloat16)
            grad_key = jnp.einsum(
                "hts,thd->shd", grad_scores, query_heads, preferred_element_type=jnp.float32
            )
            grad_value = jnp.einsum(
                "hts,thd->shd", rounded, grad_heads, preferred_element_type=jnp.float32
            )
            updated = running + jnp.einsum(
                "hts,shd->thd", grad_scores, key_rows, preferred_element_type=jnp.float32
            )
            return (
                updated,
                jnp.concatenate(
                    [grad_key.reshape(span_rows, width), grad_value.reshape(span_rows, width)],
                    axis=1,
                ),
            )

        def skipped(running):
            return (running, jnp.zeros((span_rows, 2 * width), jnp.float32))

        return lax.cond(start_pos > last_query, skipped, back_computed, grad_query)

    grad_query, key_terms = lax.scan(
        back_step, zero_query, (key_blocks, value_blocks, jnp.arange(span_count, dtype=jnp.int32))
    )
    own_terms = lax.psum_scatter(
        key_terms.reshape(row_total, 2 * width), "ctx", scatter_dimension=0, tiled=True
    )
    grad_keys = own_terms[:, :width]
    grad_values = own_terms[:, width:]
    grad_query = grad_query.reshape(row_count, width)
    grad_query_bias = jnp.sum(grad_query, axis=0)
    grad_value_bias = jnp.sum(grad_values, axis=0)
    grad_projected = jnp.concatenate([grad_query, grad_keys, grad_values], axis=1).astype(
        jnp.bfloat16
    )
    grad_qkv_weight = jnp.einsum(
        "td,te->de", normed_one, grad_projected, preferred_element_type=jnp.float32
    )
    grad_normed_one = jnp.einsum(
        "te,de->td", grad_projected, qkv_weight, preferred_element_type=jnp.float32
    )
    unused, norm_back_one = jax.vjp(layer_norm, inputs_wide, gain_one, shift_one)
    grad_inputs, grad_gain_one, grad_shift_one = norm_back_one(grad_normed_one)
    grad_inputs = grad_inputs + grad_residual
    shards = (
        lax.psum_scatter(
            grad_gain_one.astype(jnp.bfloat16), "fsdp", scatter_dimension=0, tiled=True
        ).astype(jnp.float32),
        lax.psum_scatter(
            grad_shift_one.astype(jnp.bfloat16), "fsdp", scatter_dimension=0, tiled=True
        ).astype(jnp.float32),
        lax.psum_scatter(
            grad_qkv_weight.astype(jnp.bfloat16), "fsdp", scatter_dimension=0, tiled=True
        ).astype(jnp.float32),
        lax.psum_scatter(
            grad_query_bias.astype(jnp.bfloat16), "fsdp", scatter_dimension=0, tiled=True
        ).astype(jnp.float32),
        lax.psum_scatter(
            grad_value_bias.astype(jnp.bfloat16), "fsdp", scatter_dimension=0, tiled=True
        ).astype(jnp.float32),
        lax.psum_scatter(
            grad_proj_weight.astype(jnp.bfloat16), "fsdp", scatter_dimension=0, tiled=True
        ).astype(jnp.float32),
        lax.psum_scatter(
            grad_proj_bias.astype(jnp.bfloat16), "fsdp", scatter_dimension=0, tiled=True
        ).astype(jnp.float32),
        lax.psum_scatter(
            grad_gain_two.astype(jnp.bfloat16), "fsdp", scatter_dimension=0, tiled=True
        ).astype(jnp.float32),
        lax.psum_scatter(
            grad_shift_two.astype(jnp.bfloat16), "fsdp", scatter_dimension=0, tiled=True
        ).astype(jnp.float32),
        lax.psum_scatter(
            grad_fc_weight.astype(jnp.bfloat16), "fsdp", scatter_dimension=0, tiled=True
        ).astype(jnp.float32),
        lax.psum_scatter(
            grad_fc_bias.astype(jnp.bfloat16), "fsdp", scatter_dimension=0, tiled=True
        ).astype(jnp.float32),
        lax.psum_scatter(
            grad_out_weight.astype(jnp.bfloat16), "fsdp", scatter_dimension=0, tiled=True
        ).astype(jnp.float32),
        lax.psum_scatter(
            grad_out_bias.astype(jnp.bfloat16), "fsdp", scatter_dimension=0, tiled=True
        ).astype(jnp.float32),
    )
    totals = lax.psum(
        (
            shards[0],
            shards[1],
            shards[2],
            shards[3],
            shards[4],
            shards[5],
            shards[6],
            shards[7],
            shards[8],
            shards[9],
            shards[10],
            shards[11],
            shards[12],
        ),
        "ctx",
    )
    return (
        output[None],
        grad_inputs[None],
        totals[0],
        totals[1],
        totals[2],
        totals[3],
        totals[4],
        totals[5],
        totals[6],
        totals[7],
        totals[8],
        totals[9],
        totals[10],
        totals[11],
        totals[12],
    )


def solution(mesh):
    in_specs = (
        P("fsdp", "ctx", None),
        P("fsdp", "ctx", None),
        P("fsdp"),
        P("fsdp"),
        P("fsdp", None),
        P("fsdp"),
        P("fsdp"),
        P("fsdp", None),
        P("fsdp"),
        P("fsdp"),
        P("fsdp"),
        P("fsdp", None),
        P("fsdp"),
        P("fsdp", None),
        P("fsdp"),
    )
    out_specs = (
        P("fsdp", "ctx", None),
        P("fsdp", "ctx", None),
        P("fsdp"),
        P("fsdp"),
        P("fsdp", None),
        P("fsdp"),
        P("fsdp"),
        P("fsdp", None),
        P("fsdp"),
        P("fsdp"),
        P("fsdp"),
        P("fsdp", None),
        P("fsdp"),
        P("fsdp", None),
        P("fsdp"),
    )
    return jax.shard_map(body, mesh=mesh, in_specs=in_specs, out_specs=out_specs, check_vma=False)
```

profile of v0, /device:TPU:0, one launch (start us, length us, event | category | flops | bytes accessed | tf_op | source)
XLA Modules:
  0.0 1733.6 jit_solution(4564429500221950973)
XLA Ops:
  8.7 6.2 all-gather.1
  15.6 5.8 all-gather
  24.4 41.3 %all-gather.16.cloned.1.call-done = bf16[768,2304]{1,0:T(8,128)(2,1)} async-done(((bf16[384,2304]{1,0:T(8,128)(2,1)}), bf16[768,2304]{1,0:T(8,128)(2,1)}) %all-gather.16.cloned.1.call-update) | async-done | bytes 3538960 | tf_op jit(solution)/shard_map/all_gather | solution.py:67
  69.3 5.8 all-gather.3
  75.2 5.8 all-gather.2
  83.8 5.8 all-gather.4
  89.7 5.9 all-gather.7
  95.6 5.8 all-gather.6
  101.5 5.8 all-gather.5
  107.5 79.1 %all-gather.18.cloned.1.call-done = bf16[8192,768]{1,0:T(8,128)(2,1)} async-done(((bf16[128,768]{1,0:T(8,128)(2,1)}), bf16[8192,768]{1,0:T(8,128)(2,1)}) %all-gather.18.cloned.1.call-update) | async-done | bytes 12582928 | tf_op jit(solution)/shard_map/all_gather | solution.py:113
  186.6 16.3 copy.76
  203.0 103.3 %all-gather.20.cloned.1.call-done = bf16[8192,768]{1,0:T(8,128)(2,1)} async-done(((bf16[128,768]{1,0:T(8,128)(2,1)}), bf16[8192,768]{1,0:T(8,128)(2,1)}) %all-gather.20.cloned.1.call-update) | async-done | bytes 12582928 | tf_op jit(solution)/shard_map/all_gather | solution.py:114
  306.2 15.8 copy.77
  322.1 5.7 while.34
  322.2 4.4 conditional.6
  327.9 6.2 all-gather.22.cloned.1.call-done
  336.0 65.6 %all-gather.24.cloned.1.call-done = bf16[768,3072]{1,0:T(8,128)(2,1)} async-done(((bf16[384,3072]{1,0:T(8,128)(2,1)}), bf16[768,3072]{1,0:T(8,128)(2,1)}) %all-gather.24.cloned.1.call-update) | async-done | bytes 4718608 | tf_op jit(solution)/shard_map/all_gather | solution.py:74
  404.9 64.3 %all-gather.26.cloned.1.call-done = bf16[3072,768]{1,0:T(8,128)(2,1)} async-done(((bf16[1536,768]{1,0:T(8,128)(2,1)}), bf16[3072,768]{1,0:T(8,128)(2,1)}) %all-gather.26.cloned.1.call-update) | async-done | bytes 4718608 | tf_op jit(solution)/shard_map/all_gather | solution.py:76
  469.2 5.4 fusion.95
  477.3 9.5 copy.108
  486.9 18.8 %copy.81 = bf16[16,512,12,64]{1,3,2,0:T(8,128)(2,1)} copy(bf16[16,512,12,64]{1,0,3,2:T(8,128)(2,1)S(1)} %bitcast.175) | data formatting | bytes 25165824
  506.3 4.6 copy.109
  510.9 18.6 %copy.82 = bf16[16,512,12,64]{1,3,2,0:T(8,128)(2,1)} copy(bf16[16,512,12,64]{1,0,3,2:T(8,128)(2,1)S(1)} %bitcast.176) | data formatting | bytes 25165824
  532.7 134.6 %while.35 = (s32[]{:T(128)}, f32[128,12,64]{0,2,1:T(8,128)}, f32[16,512,1536]{2,1,0:T(8,128)}, s32[16]{0:T(128)S(1)}, s32[]{:T(128)}, /*index=5*/bf16[16,512,12,...) while((s32[]{:T(128)}, f32[128,12,64]{0,2,1:T(8,128)}, ...), condition=%wide.region_16.17_spmd.clone, body=%wide.region_13.16_spmd.clone.sunk | while | flops 514491008 | bytes 40333600 | solution.py:259
  533.9 10.1 conditional.7
  546.4 3.7 constant_dynamic-update-slice_fusion.2
  554.1 3.8 constant_dynamic-update-slice_fusion.2
  562.0 3.8 constant_dynamic-update-slice_fusion.2
  569.8 3.7 constant_dynamic-update-slice_fusion.2
  577.6 3.7 constant_dynamic-update-slice_fusion.2
  585.3 3.7 constant_dynamic-update-slice_fusion.2
  593.1 3.8 constant_dynamic-update-slice_fusion.2
  600.9 3.8 constant_dynamic-update-slice_fusion.2
  608.7 3.8 constant_dynamic-update-slice_fusion.2
  616.6 3.8 constant_dynamic-update-slice_fusion.2
  632.2 3.8 constant_dynamic-update-slice_fusion.2
  647.8 3.8 constant_dynamic-update-slice_fusion.2
  655.6 3.8 constant_dynamic-update-slice_fusion.2
  675.2 3.8 convolution_convert_fusion
  680.5 502.5 %reduce-scatter.6.cloned.1.call-done = f32[128,1536]{1,0:T(8,128)} async-done(((f32[8192,1536]{1,0:T(8,128)}), f32[128,1536]{1,0:T(8,128)}) %reduce-scatter.6.cloned.1.call-update) | async-done | bytes 786448 | tf_op jit(solution)/shard_map/reduce_scatter | solution.py:262
  1188.5 5.8 all-gather.8
  1198.1 4.1 fusion.55
  1202.3 7.9 reduce-scatter.10.cloned.1.call-done
  1210.2 66.5 %reduce-scatter.12.cloned.1.call-done = bf16[384,3072]{1,0:T(8,128)(2,1)} async-done(((bf16[768,3072]{1,0:T(8,128)(2,1)}), bf16[384,3072]{1,0:T(8,128)(2,1)}) %reduce-scatter.12.cloned.1.call-update) | async-done | bytes 2359312 | tf_op jit(solution)/shard_map/reduce_scatter | solution.py:310
  1276.7 66.2 %reduce-scatter.14.cloned.1.call-done = bf16[1536,768]{1,0:T(8,128)(2,1)} async-done(((bf16[3072,768]{1,0:T(8,128)(2,1)}), bf16[1536,768]{1,0:T(8,128)(2,1)}) %reduce-scatter.14.cloned.1.call-update) | async-done | bytes 2359312 | tf_op jit(solution)/shard_map/reduce_scatter | solution.py:316
  1348.1 8.4 all-reduce.10
  1356.9 40.2 %reduce-scatter.8.cloned.1.call-done = bf16[384,2304]{1,0:T(8,128)(2,1)} async-done(((bf16[768,2304]{1,0:T(8,128)(2,1)}), bf16[384,2304]{1,0:T(8,128)(2,1)}) %reduce-scatter.8.cloned.1.call-update) | async-done | bytes 1769488 | tf_op jit(solution)/shard_map/reduce_scatter | solution.py:289
  1397.1 330.0 %all-reduce.12 = (f32[384]{0:T(512)}, f32[384]{0:T(512)}, f32[384,2304]{1,0:T(8,128)}, f32[384]{0:T(512)}, f32[384]{0:T(512)}, /*index=5*/f32[384,768]{1,0:T(8,1...) all-reduce(f32[384]{0:T(512)S(1)} %get-tuple-element.680, ...), channel_id=1, replica_groups=mesh['ctx'=64,'fsdp'=2] {'ctx'}, use_global_device_ids=true, to_apply=%region_22.23 | all-reduce | flops 3543552 | bytes 21270528 | tf_op jit(solution)/shard_map/psum | solution.py:323
  (380 shorter events, 131.0 us)
Async XLA Ops:
  7.2 58.5 %all-gather.16.cloned.1.call-start = ((), (), s32[]{:S(2)}) async-start(), calls=%async_computation.5 | async-start | bytes 5308416 | tf_op jit(solution)/shard_map/all_gather | solution.py:67
  7.9 61.4 %copy-start.47 = (bf16[384]{0:T(512)(128)(2,1)S(1)}, bf16[384]{0:T(512)(128)(2,1)}, u32[]{:S(2)}) copy-start(bf16[384]{0:T(512)(128)(2,1)} %param.29) | copy-start | bytes 2308
  7.9 67.3 %copy-start.48 = (bf16[384]{0:T(512)(128)(2,1)S(1)}, bf16[384]{0:T(512)(128)(2,1)}, u32[]{:S(2)}) copy-start(bf16[384]{0:T(512)(128)(2,1)} %param.28) | copy-start | bytes 2308
  7.9 178.7 %all-gather.18.cloned.1.call-start = ((), (), s32[]{:S(2)}) async-start(), calls=%async_computation.6 | async-start | bytes 12779520 | tf_op jit(solution)/shard_map/all_gather | solution.py:113
  14.9 66.2 %copy-start.26 = (f32[768]{0:T(1024)}, f32[768]{0:T(1024)S(1)}, u32[]{:S(2)}) copy-start(f32[768]{0:T(1024)S(1)} %reshape.253) | copy-start | bytes 9220
  21.5 59.6 %copy-start.19 = (f32[768]{0:T(1024)}, f32[768]{0:T(1024)S(1)}, u32[]{:S(2)}) copy-start(f32[768]{0:T(1024)S(1)} %reshape.252) | copy-start | bytes 9220
  22.6 58.5 %copy-start.31 = (f32[128]{0:T(128)}, f32[128]{0:T(128)S(1)}, u32[]{:S(2)}) copy-start(f32[128]{0:T(128)S(1)} %broadcast_multiply_fusion.1) | copy-start | bytes 1540
  24.4 56.7 %copy-start.36 = (f32[128]{0:T(128)}, f32[128]{0:T(128)S(1)}, u32[]{:S(2)}) copy-start(f32[128]{0:T(128)S(1)} %fusion.82) | copy-start | bytes 1540
  69.3 237.0 %all-gather.20.cloned.1.call-start = ((), (), s32[]{:S(2)}) async-start(), calls=%async_computation.7 | async-start | bytes 12779520 | tf_op jit(solution)/shard_map/all_gather | solution.py:114
  81.1 8.5 copy-start.46
  81.2 14.4 copy-start.50
  81.2 20.3 %copy-start.51 = (bf16[384]{0:T(512)(128)(2,1)S(1)}, bf16[384]{0:T(512)(128)(2,1)}, u32[]{:S(2)}) copy-start(bf16[384]{0:T(512)(128)(2,1)} %param.32) | copy-start | bytes 2308
  81.9 252.1 %all-gather.22.cloned.1.call-start = ((), (), s32[]{:S(2)}) async-start(), calls=%async_computation.8 | async-start | bytes 1769472 | tf_op jit(solution)/shard_map/all_gather | solution.py:70
  82.5 319.1 %all-gather.24.cloned.1.call-start = ((), (), s32[]{:S(2)}) async-start(), calls=%async_computation.9 | async-start | bytes 7077888 | tf_op jit(solution)/shard_map/all_gather | solution.py:74
  83.1 386.1 %all-gather.26.cloned.1.call-start = ((), (), s32[]{:S(2)}) async-start(), calls=%async_computation.10 | async-start | bytes 7077888 | tf_op jit(solution)/shard_map/all_gather | solution.py:76
  83.7 1099.3 %reduce-scatter.6.cloned.1.call-start = ((), (), s32[]{:S(2)}) async-start(), calls=%async_computation.11 | async-start | bytes 51118080 | tf_op jit(solution)/shard_map/reduce_scatter | solution.py:262
  101.5 300.2 %copy-start.24 = (f32[768]{0:T(1024)}, f32[768]{0:T(1024)S(1)}, u32[]{:S(2)}) copy-start(f32[768]{0:T(1024)S(1)} %reshape.258) | copy-start | bytes 9220
  107.4 294.3 %copy-start.21 = (f32[768]{0:T(1024)}, f32[768]{0:T(1024)S(1)}, u32[]{:S(2)}) copy-start(f32[768]{0:T(1024)S(1)} %reshape.257) | copy-start | bytes 9220
  322.1 12.0 copy-start.5
  327.9 202.9 %copy-start.11 = (bf16[128,12,64]{0,2,1:T(8,128)(2,1)}, bf16[128,12,64]{0,2,1:T(8,128)(2,1)S(1)}, u32[]{:S(2)}) copy-start(bf16[128,12,64]{0,2,1:T(8,128)(2,1)S(1)} %divide_convert_fusion) | copy-start | bytes 589828
  335.8 141.2 %copy-start.1 = (f32[128,768]{1,0:T(8,128)}, f32[128,768]{1,0:T(8,128)S(1)}, u32[]{:S(2)}) copy-start(f32[128,768]{1,0:T(8,128)S(1)} %get-tuple-element.668) | copy-start | bytes 1179652
  335.8 69.1 %copy-start.28 = (f32[128]{0:T(128)}, f32[128]{0:T(128)S(1)}, u32[]{:S(2)}) copy-start(f32[128]{0:T(128)S(1)} %broadcast_multiply_fusion) | copy-start | bytes 1540
  336.0 68.9 %copy-start.55 = (f32[128]{0:T(128)}, f32[128]{0:T(128)S(1)}, u32[]{:S(2)}) copy-start(f32[128]{0:T(128)S(1)} %multiply_reduce_fusion.2) | copy-start | bytes 1540
  336.0 68.9 %copy-start.33 = (f32[128]{0:T(128)}, f32[128]{0:T(128)S(1)}, u32[]{:S(2)}) copy-start(f32[128]{0:T(128)S(1)} %fusion.83) | copy-start | bytes 1540
  401.6 67.6 %copy-start.8 = (bf16[1,128,768]{2,1,0:T(8,128)(2,1)S(1)}, bf16[1,128,768]{2,1,0:T(8,128)(2,1)}, u32[]{:S(2)}) copy-start(bf16[1,128,768]{2,1,0:T(8,128)(2,1)} %param.24) | copy-start | bytes 589828
  404.9 69.7 %copy-start.3 = (f32[128,3072]{1,0:T(8,128)}, f32[128,3072]{1,0:T(8,128)S(1)}, u32[]{:S(2)}) copy-start(f32[128,3072]{1,0:T(8,128)S(1)} %convolution_add_fusion) | copy-start | bytes 4718596
  469.2 5.4 copy-start.29
  469.2 5.4 copy-start.34
  477.3 52.2 %copy-start.6 = (f32[128,768]{1,0:T(8,128)}, f32[128,768]{1,0:T(8,128)S(1)}, u32[]{:S(2)}) copy-start(f32[128,768]{1,0:T(8,128)S(1)} %get-tuple-element.656) | copy-start | bytes 1179652
  477.3 52.2 %copy-start.43 = (f32[128]{0:T(128)}, f32[128]{0:T(128)S(1)}, u32[]{:S(2)}) copy-start(f32[128]{0:T(128)S(1)} %negate_multiply_fusion.1) | copy-start | bytes 1540
  486.8 19.4 %slice-start = ((s8[12582912]{0:T(1024)(128)(4,1)}), s8[4194304]{0:T(1024)(128)(4,1)S(1)}, s32[]{:S(2)}) async-start(s8[12582912]{0:T(1024)(128)(4,1)} %bitcast.169), calls=%async_computation.16 | async-start | bytes 8388608
  486.8 19.4 %slice-start.1 = ((s8[12582912]{0:T(1024)(128)(4,1)}), s8[4194304]{0:T(1024)(128)(4,1)S(1)}, s32[]{:S(2)}) async-start(s8[12582912]{0:T(1024)(128)(4,1)} %bitcast.169), calls=%async_computation.17 | async-start | bytes 8388608
  486.9 19.4 %slice-start.2 = ((s8[12582912]{0:T(1024)(128)(4,1)}), s8[4194304]{0:T(1024)(128)(4,1)S(1)}, s32[]{:S(2)}) async-start(s8[12582912]{0:T(1024)(128)(4,1)} %bitcast.169), calls=%async_computation.18 | async-start | bytes 8388608
  510.9 18.6 %copy-start.10 = (bf16[768,768]{1,0:T(8,128)(2,1)S(1)}, bf16[768,768]{1,0:T(8,128)(2,1)}, u32[]{:S(2)}) copy-start(bf16[768,768]{1,0:T(8,128)(2,1)} %all-gather.22.cloned.1.call-done) | copy-start | bytes 3538948
  667.3 542.8 %reduce-scatter.10.cloned.1.call-start = ((), (), s32[]{:S(2)}) async-start(), calls=%async_computation.13 | async-start | bytes 1769472 | tf_op jit(solution)/shard_map/reduce_scatter | solution.py:298
  669.9 606.8 %reduce-scatter.12.cloned.1.call-start = ((), (), s32[]{:S(2)}) async-start(), calls=%async_computation.14 | async-start | bytes 7077888 | tf_op jit(solution)/shard_map/reduce_scatter | solution.py:310
  673.8 669.2 %reduce-scatter.14.cloned.1.call-start = ((), (), s32[]{:S(2)}) async-start(), calls=%async_computation.15 | async-start | bytes 7077888 | tf_op jit(solution)/shard_map/reduce_scatter | solution.py:316
  679.0 505.2 %copy-start.20 = (f32[768]{0:T(1024)S(1)}, f32[768]{0:T(1024)}, u32[]{:S(2)}) copy-start(f32[768]{0:T(1024)} %copy-done.19) | copy-start | bytes 9220
  679.0 505.2 %copy-start.27 = (f32[768]{0:T(1024)S(1)}, f32[768]{0:T(1024)}, u32[]{:S(2)}) copy-start(f32[768]{0:T(1024)} %copy-done.26) | copy-start | bytes 9220
  679.0 505.2 %copy-start.32 = (f32[128]{0:T(128)S(1)}, f32[128]{0:T(128)}, u32[]{:S(2)}) copy-start(f32[128]{0:T(128)} %copy-done.31) | copy-start | bytes 1540
  679.0 718.1 %reduce-scatter.8.cloned.1.call-start = ((), (), s32[]{:S(2)}) async-start(), calls=%async_computation.12 | async-start | bytes 5308416 | tf_op jit(solution)/shard_map/reduce_scatter | solution.py:289
  680.5 507.3 %copy-start.17 = (bf16[128,768]{1,0:T(8,128)(2,1)}, bf16[128,768]{1,0:T(8,128)(2,1)S(1)}, u32[]{:S(2)}) copy-start(bf16[128,768]{1,0:T(8,128)(2,1)S(1)} %copy.84) | copy-start | bytes 589828
  1187.8 7.8 copy-start.57
  1198.1 144.8 %copy-start.15 = (f32[128,1536]{1,0:T(8,128)S(1)}, f32[128,1536]{1,0:T(8,128)}, u32[]{:S(2)}) copy-start(f32[128,1536]{1,0:T(8,128)} %reduce-scatter.6.cloned.1.call-done) | copy-start | bytes 2359300
  1202.3 144.4 %copy-start.54 = (f32[128]{0:T(128)S(1)}, f32[128]{0:T(128)}, u32[]{:S(2)}) copy-start(f32[128]{0:T(128)} %copy-done.53) | copy-start | bytes 1540
  1202.3 144.5 %copy-start.37 = (f32[128]{0:T(128)S(1)}, f32[128]{0:T(128)}, u32[]{:S(2)}) copy-start(f32[128]{0:T(128)} %copy-done.36) | copy-start | bytes 1540
  1202.3 144.8 %copy-start.45 = (f32[128]{0:T(128)S(1)}, f32[128]{0:T(128)}, u32[]{:S(2)}) copy-start(f32[128]{0:T(128)} %copy-done.43) | copy-start | bytes 1540
  1343.0 54.0 %copy-start.18 = (bf16[384,768]{1,0:T(8,128)(2,1)S(1)}, bf16[384,768]{1,0:T(8,128)(2,1)}, u32[]{:S(2)}) copy-start(bf16[384,768]{1,0:T(8,128)(2,1)} %reduce-scatter.10.cloned.1.call-done) | copy-start | bytes 1769476
  (24 other events, 70.4 us)
Sparse Core Ops, SparseCore 0:
  9.7 56.0 all-gather.15
  69.4 117.2 all-gather.17
  188.9 117.2 all-gather.19
  307.7 26.2 all-gather.21
  335.6 66.0 all-gather.23
  403.1 66.0 all-gather.25
  667.4 515.5 reduce-scatter.5
  1185.9 24.1 reduce-scatter.9
  1213.3 63.3 reduce-scatter.11
  1279.5 63.3 reduce-scatter.13
  1346.0 51.0 reduce-scatter.7
where the time goes:
time: 1740 us; the launch traced here: 1730 us
  waiting for transfers between devices  1050 us (60%)
  blocking collectives  391 us (22%)
  local copies, waits for them, and re-layouts  208 us (12%)
  matrix products  48 us (3%)
    reduce_scatter x1, waiting for transfers between devices, body(): lax.psum_scatter(key_terms.reshape(row_total, 2 * width), 'ctx', scatter_...  503 us
    psum x1, blocking collectives, body(): lax.psum((shards[0], shards[1], shards[2], shards[3], shards[4], shards[5...  330 us
    all_gather x1, waiting for transfers between devices, body(): value_span = lax.all_gather(values_local, 'ctx', axis=0, tiled=True)  103 us
    dynamic_update_slice x32, local copies, waits for them, and re-layouts, body(): lax.scan(back_step, zero_query, (key_blocks, value_blocks, jnp.arange(spa...  98.1 us
    unnamed x138, local copies, waits for them, and re-layouts  89.2 us
    all_gather x1, waiting for transfers between devices, body(): key_span = lax.all_gather(keys_local, 'ctx', axis=0, tiled=True)  79.1 us
    reduce_scatter x1, waiting for transfers between devices, body(): lax.psum_scatter(grad_fc_weight.astype(jnp.bfloat16), 'fsdp', scatter_dim...  66.5 us
    reduce_scatter x1, waiting for transfers between devices, body(): lax.psum_scatter(grad_out_weight.astype(jnp.bfloat16), 'fsdp', scatter_di...  66.2 us
  transfers between devices with their start and end apart: 11, of which 11 were waited for; matrix products, arithmetic and copies ran while one was open for 4% of the time, Pallas kernels for 0%

commit v1 on v0

--- a/solution.py
+++ b/solution.py
@@ -111,7 +111,9 @@
         jnp.zeros((row_count, head_count, head_width), jnp.float32),
     )
     key_span = lax.all_gather(keys_local, "ctx", axis=0, tiled=True)
-    value_span = lax.all_gather(values_local, "ctx", axis=0, tiled=True)
+    value_span = jnp.concatenate(
+        lax.all_to_all(jnp.stack([values_local] * lax.axis_size("ctx")), "ctx", 0, 0), axis=0
+    )
     span_total = key_span.shape[0]
     attend_span_rows = math.gcd(span_total, 512)
 

time: 1740 us -> 1870 us (1.075)
  blocking collectives: 391 us -> 488 us
  local copies, waits for them, and re-layouts: 208 us -> 256 us
  waiting for transfers between devices: 1050 us -> 1020 us
    all_to_all x0 -> x1, waiting for transfers between devices: none -> 80 us  [body(): lax.all_to_all(jnp.stack([values_local] * lax.axis_size('ctx')), 'ctx', 0...]
    all_gather x1, waiting for transfers between devices: 79.1 us -> 0.01 us  [body(): key_span = lax.all_gather(keys_local, 'ctx', axis=0, tiled=True)]
    all_gather x1, blocking collectives: 5.84 us -> 71 us  [body(): lax.all_gather(b_proj, 'fsdp', axis=0, tiled=True)]
    all_gather x1, blocking collectives: 5.87 us -> 33.9 us  [body(): lax.all_gather(b_fc, 'fsdp', axis=0, tiled=True)]
    all_gather x1, waiting for transfers between devices: 65.6 us -> 38.7 us  [body(): lax.all_gather(w_fc, 'fsdp', axis=0, tiled=True)]
    unnamed x138 -> x132, local copies, waits for them, and re-layouts: 89.2 us -> 95.8 us
  transfers between devices with their start and end apart: 11 -> 12, of which waited for: 11 -> 10; matrix products, arithmetic and copies ran while one was open for 4% -> 7% of each run, Pallas kernels for 0% -> 0%
where the time goes in v1:
time: 1870 us; the launch traced here: 1860 us
  waiting for transfers between devices  1020 us (55%)
  blocking collectives  488 us (26%)
  local copies, waits for them, and re-layouts  256 us (14%)
  matrix products  48 us (3%)
    reduce_scatter x1, waiting for transfers between devices, body(): lax.psum_scatter(key_terms.reshape(row_total, 2 * width), 'ctx', scatter_...  501 us
    psum x1, blocking collectives, body(): lax.psum((shards[0], shards[1], shards[2], shards[3], shards[4], shards[5...  330 us
    all_gather x1, waiting for transfers between devices, body(): lax.all_gather(values_local, 'ctx', axis=0, tiled=True)  111 us
    dynamic_update_slice x32, local copies, waits for them, and re-layouts, body(): lax.scan(back_step, zero_query, (key_blocks, value_blocks, jnp.arange(spa...  98 us
    unnamed x132, local copies, waits for them, and re-layouts  95.8 us
    all_to_all x1, waiting for transfers between devices, body(): lax.all_to_all(jnp.stack([values_local] * lax.axis_size('ctx')), 'ctx', 0...  80 us
    all_gather x1, blocking collectives, body(): lax.all_gather(b_proj, 'fsdp', axis=0, tiled=True)  71 us
    reduce_scatter x1, waiting for transfers between devices, body(): lax.psum_scatter(grad_fc_weight.astype(jnp.bfloat16), 'fsdp', scatter_dim...  66.5 us
  transfers between devices with their start and end apart: 12, of which 10 were waited for; matrix products, arithmetic and copies ran while one was open for 7% of the time, Pallas kernels for 0%

profile of v1, /device:TPU:0, one launch (start us, length us, event | category | flops | bytes accessed | tf_op | source)
XLA Modules:
  0.0 1860.9 jit_solution(8911359809033441323)
XLA Ops:
  8.6 6.2 all-gather.1
  15.6 5.8 all-gather
  24.3 41.4 %all-gather.16.cloned.1.call-done = bf16[768,2304]{1,0:T(8,128)(2,1)} async-done(((bf16[384,2304]{1,0:T(8,128)(2,1)}), bf16[768,2304]{1,0:T(8,128)(2,1)}) %all-gather.16.cloned.1.call-update) | async-done | bytes 3538960 | tf_op jit(solution)/shard_map/all_gather | solution.py:67
  71.3 5.8 all-gather.3
  77.2 5.8 all-gather.2
  84.9 7.6 stack.2
  92.5 8.2 all-to-all-start
  100.8 71.0 %all-gather.4 = bf16[2,1,384]{2,1,0:T(2,128)(2,1)S(1)} all-gather(bf16[1,1,384]{2,1,0:T(2,128)(2,1)S(1)} %reshape.248), channel_id=1, replica_groups=mesh['ctx'=64,'fsdp'=2] {'fsdp'}, dimensions={0}, use_global_device_ids=true | all-gather | bytes 2304 | tf_op jit(solution)/shard_map/all_gather | solution.py:71
  171.9 33.9 %all-gather.7 = bf16[2,1,1536]{2,1,0:T(2,128)(2,1)S(1)} all-gather(bf16[1,1,1536]{2,1,0:T(2,128)(2,1)S(1)} %reshape.254), channel_id=1, replica_groups=mesh['ctx'=64,'fsdp'=2] {'fsdp'}, dimensions={0}, use_global_device_ids=true | all-gather | bytes 9216 | tf_op jit(solution)/shard_map/all_gather | solution.py:75
  205.8 6.0 all-gather.6
  211.8 8.7 all-gather.5
  220.7 80.0 %all-to-all-done = bf16[64,128,768]{1,2,0:T(8,128)(2,1)} async-done(((bf16[64,128,768]{1,2,0:T(8,128)(2,1)}), bf16[64,128,768]{1,2,0:T(8,128)(2,1)}, u32[]{:S(2)}, u32[]{:S(2)}) %all-to-all-start) | async-done | bytes 12582944 | tf_op jit(solution)/shard_map/all_to_all | solution.py:115
  300.8 16.7 copy.91
  317.5 16.7 copy.93
  334.2 16.8 copy.92
  351.0 5.7 while.34
  351.1 4.4 conditional.6
  356.8 9.5 copy.124
  366.3 19.1 %copy.97 = bf16[16,512,12,64]{1,3,2,0:T(8,128)(2,1)} copy(bf16[16,512,12,64]{1,0,3,2:T(8,128)(2,1)S(1)} %bitcast.174) | data formatting | bytes 25165824
  387.4 38.7 %all-gather.22.cloned.1.call-done = bf16[768,3072]{1,0:T(8,128)(2,1)} async-done(((bf16[384,3072]{1,0:T(8,128)(2,1)}), bf16[768,3072]{1,0:T(8,128)(2,1)}) %all-gather.22.cloned.1.call-update) | async-done | bytes 4718608 | tf_op jit(solution)/shard_map/all_gather | solution.py:74
  429.4 64.3 %all-gather.24.cloned.1.call-done = bf16[3072,768]{1,0:T(8,128)(2,1)} async-done(((bf16[1536,768]{1,0:T(8,128)(2,1)}), bf16[3072,768]{1,0:T(8,128)(2,1)}) %all-gather.24.cloned.1.call-update) | async-done | bytes 4718608 | tf_op jit(solution)/shard_map/all_gather | solution.py:76
  493.7 5.4 fusion.95
  502.5 110.7 %all-gather.26.cloned.1.call-done = bf16[8192,768]{1,0:T(8,128)(2,1)} async-done(((bf16[128,768]{1,0:T(8,128)(2,1)}), bf16[8192,768]{1,0:T(8,128)(2,1)}) %all-gather.26.cloned.1.call-update) | async-done | bytes 12582928 | tf_op jit(solution)/shard_map/all_gather | solution.py:213
  613.2 16.1 copy.95
  629.3 9.4 copy.125
  638.7 18.6 copy.98
  660.5 134.6 %while.35 = (s32[]{:T(128)}, f32[128,12,64]{0,2,1:T(8,128)}, f32[16,512,1536]{2,1,0:T(8,128)}, s32[16]{0:T(128)S(1)}, s32[]{:T(128)}, /*index=5*/bf16[16,512,12,...) while((s32[]{:T(128)}, f32[128,12,64]{0,2,1:T(8,128)}, ...), condition=%wide.region_16.17_spmd.clone, body=%wide.region_13.16_spmd.clone.sunk | while | flops 514491008 | bytes 40333600 | solution.py:261
  661.9 10.1 conditional.7
  682.1 3.8 constant_dynamic-update-slice_fusion.2
  689.9 3.8 constant_dynamic-update-slice_fusion.2
  697.8 3.7 constant_dynamic-update-slice_fusion.2
  721.1 3.8 constant_dynamic-update-slice_fusion.2
  728.9 3.8 constant_dynamic-update-slice_fusion.2
  736.7 3.8 constant_dynamic-update-slice_fusion.2
  744.5 3.8 constant_dynamic-update-slice_fusion.2
  760.1 3.8 constant_dynamic-update-slice_fusion.2
  775.7 3.8 constant_dynamic-update-slice_fusion.2
  783.5 3.8 constant_dynamic-update-slice_fusion.2
  803.1 3.8 convolution_convert_fusion
  808.4 501.4 %reduce-scatter.6.cloned.1.call-done = f32[128,1536]{1,0:T(8,128)} async-done(((f32[8192,1536]{1,0:T(8,128)}), f32[128,1536]{1,0:T(8,128)}) %reduce-scatter.6.cloned.1.call-update) | async-done | bytes 786448 | tf_op jit(solution)/shard_map/reduce_scatter | solution.py:264
  1315.3 6.0 all-gather.8
  1325.2 4.1 fusion.55
  1329.3 7.9 reduce-scatter.10.cloned.1.call-done
  1337.3 66.5 %reduce-scatter.12.cloned.1.call-done = bf16[384,3072]{1,0:T(8,128)(2,1)} async-done(((bf16[768,3072]{1,0:T(8,128)(2,1)}), bf16[384,3072]{1,0:T(8,128)(2,1)}) %reduce-scatter.12.cloned.1.call-update) | async-done | bytes 2359312 | tf_op jit(solution)/shard_map/reduce_scatter | solution.py:312
  1403.8 66.3 %reduce-scatter.14.cloned.1.call-done = bf16[1536,768]{1,0:T(8,128)(2,1)} async-done(((bf16[3072,768]{1,0:T(8,128)(2,1)}), bf16[1536,768]{1,0:T(8,128)(2,1)}) %reduce-scatter.14.cloned.1.call-update) | async-done | bytes 2359312 | tf_op jit(solution)/shard_map/reduce_scatter | solution.py:318
  1475.2 8.4 all-reduce.10
  1484.0 40.2 %reduce-scatter.8.cloned.1.call-done = bf16[384,2304]{1,0:T(8,128)(2,1)} async-done(((bf16[768,2304]{1,0:T(8,128)(2,1)}), bf16[384,2304]{1,0:T(8,128)(2,1)}) %reduce-scatter.8.cloned.1.call-update) | async-done | bytes 1769488 | tf_op jit(solution)/shard_map/reduce_scatter | solution.py:291
  1524.2 330.0 %all-reduce.12 = (f32[384]{0:T(512)}, f32[384]{0:T(512)}, f32[384,2304]{1,0:T(8,128)}, f32[384]{0:T(512)}, f32[384]{0:T(512)}, /*index=5*/f32[384,768]{1,0:T(8,1...) all-reduce(f32[384]{0:T(512)S(1)} %get-tuple-element.701, ...), channel_id=1, replica_groups=mesh['ctx'=64,'fsdp'=2] {'ctx'}, use_global_device_ids=true, to_apply=%region_22.23 | all-reduce | flops 3543552 | bytes 21270528 | tf_op jit(solution)/shard_map/psum | solution.py:325
  (379 shorter events, 143.6 us)
Async XLA Ops:
  7.2 58.5 %all-gather.16.cloned.1.call-start = ((), (), s32[]{:S(2)}) async-start(), calls=%async_computation.6 | async-start | bytes 5308416 | tf_op jit(solution)/shard_map/all_gather | solution.py:67
  7.9 326.3 %all-gather.18.cloned.1.call-start = ((), (), s32[]{:S(2)}) async-start(), calls=%async_computation.7 | async-start | bytes 12779520 | tf_op jit(solution)/shard_map/all_gather | solution.py:113
  14.9 55.1 %copy-start.26 = (f32[768]{0:T(1024)}, f32[768]{0:T(1024)S(1)}, u32[]{:S(2)}) copy-start(f32[768]{0:T(1024)S(1)} %reshape.259) | copy-start | bytes 9220
  21.5 48.6 %copy-start.19 = (f32[768]{0:T(1024)}, f32[768]{0:T(1024)S(1)}, u32[]{:S(2)}) copy-start(f32[768]{0:T(1024)S(1)} %reshape.258) | copy-start | bytes 9220
  22.6 47.5 %copy-start.31 = (f32[128]{0:T(128)}, f32[128]{0:T(128)S(1)}, u32[]{:S(2)}) copy-start(f32[128]{0:T(128)S(1)} %broadcast_multiply_fusion.1) | copy-start | bytes 1540
  24.3 46.3 %copy-start.36 = (f32[128]{0:T(128)}, f32[128]{0:T(128)S(1)}, u32[]{:S(2)}) copy-start(f32[128]{0:T(128)S(1)} %fusion.82) | copy-start | bytes 1540
  68.5 8.6 copy-start.48
  69.3 316.1 %all-gather.20.cloned.1.call-start = ((), (), s32[]{:S(2)}) async-start(), calls=%async_computation.8 | async-start | bytes 1769472 | tf_op jit(solution)/shard_map/all_gather | solution.py:70
  70.0 356.1 %all-gather.22.cloned.1.call-start = ((), (), s32[]{:S(2)}) async-start(), calls=%async_computation.9 | async-start | bytes 7077888 | tf_op jit(solution)/shard_map/all_gather | solution.py:74
  70.6 423.1 %all-gather.24.cloned.1.call-start = ((), (), s32[]{:S(2)}) async-start(), calls=%async_computation.10 | async-start | bytes 7077888 | tf_op jit(solution)/shard_map/all_gather | solution.py:76
  71.2 542.0 %all-gather.26.cloned.1.call-start = ((), (), s32[]{:S(2)}) async-start(), calls=%async_computation.11 | async-start | bytes 12779520 | tf_op jit(solution)/shard_map/all_gather | solution.py:213
  92.5 8.2 copy-start.49
  92.5 79.3 %copy-start.46 = (bf16[1536]{0:T(1024)(128)(2,1)S(1)}, bf16[1536]{0:T(1024)(128)(2,1)}, u32[]{:S(2)}) copy-start(bf16[1536]{0:T(1024)(128)(2,1)} %param.35) | copy-start | bytes 9220
  92.5 113.3 %copy-start.50 = (bf16[384]{0:T(512)(128)(2,1)S(1)}, bf16[384]{0:T(512)(128)(2,1)}, u32[]{:S(2)}) copy-start(bf16[384]{0:T(512)(128)(2,1)} %param.33) | copy-start | bytes 2308
  92.5 119.3 %copy-start.51 = (bf16[384]{0:T(512)(128)(2,1)S(1)}, bf16[384]{0:T(512)(128)(2,1)}, u32[]{:S(2)}) copy-start(bf16[384]{0:T(512)(128)(2,1)} %param.32) | copy-start | bytes 2308
  92.5 208.2 %all-to-all-start = ((bf16[64,128,768]{1,2,0:T(8,128)(2,1)}), bf16[64,128,768]{1,2,0:T(8,128)(2,1)}, u32[]{:S(2)}, u32[]{:S(2)}) async-start(bf16[64,128,768]{1,2,0:T(8,128)(2,1)} %stack.2), calls=%async_computation | async-start | bytes 25165824 | tf_op jit(solution)/shard_map/all_to_all | solution.py:115
  100.7 1209.1 %reduce-scatter.6.cloned.1.call-start = ((), (), s32[]{:S(2)}) async-start(), calls=%async_computation.12 | async-start | bytes 51118080 | tf_op jit(solution)/shard_map/reduce_scatter | solution.py:264
  211.8 214.3 %copy-start.24 = (f32[768]{0:T(1024)}, f32[768]{0:T(1024)S(1)}, u32[]{:S(2)}) copy-start(f32[768]{0:T(1024)S(1)} %reshape.264) | copy-start | bytes 9220
  220.6 205.6 %copy-start.21 = (f32[768]{0:T(1024)}, f32[768]{0:T(1024)S(1)}, u32[]{:S(2)}) copy-start(f32[768]{0:T(1024)S(1)} %reshape.263) | copy-start | bytes 9220
  356.8 301.8 %copy-start.11 = (bf16[128,12,64]{0,2,1:T(8,128)(2,1)}, bf16[128,12,64]{0,2,1:T(8,128)(2,1)S(1)}, u32[]{:S(2)}) copy-start(bf16[128,12,64]{0,2,1:T(8,128)(2,1)S(1)} %divide_convert_fusion) | copy-start | bytes 589828
  366.3 19.1 %copy-start.5 = (bf16[1,128,768]{2,1,0:T(8,128)(2,1)S(1)}, bf16[1,128,768]{2,1,0:T(8,128)(2,1)}, u32[]{:S(2)}) copy-start(bf16[1,128,768]{2,1,0:T(8,128)(2,1)} %param.23) | copy-start | bytes 589828
  387.2 114.4 %copy-start.1 = (f32[128,768]{1,0:T(8,128)}, f32[128,768]{1,0:T(8,128)S(1)}, u32[]{:S(2)}) copy-start(f32[128,768]{1,0:T(8,128)S(1)} %get-tuple-element.689) | copy-start | bytes 1179652
  387.2 42.2 %copy-start.28 = (f32[128]{0:T(128)}, f32[128]{0:T(128)S(1)}, u32[]{:S(2)}) copy-start(f32[128]{0:T(128)S(1)} %broadcast_multiply_fusion) | copy-start | bytes 1540
  387.4 42.0 %copy-start.55 = (f32[128]{0:T(128)}, f32[128]{0:T(128)S(1)}, u32[]{:S(2)}) copy-start(f32[128]{0:T(128)S(1)} %multiply_reduce_fusion.2) | copy-start | bytes 1540
  387.4 42.0 %copy-start.33 = (f32[128]{0:T(128)}, f32[128]{0:T(128)S(1)}, u32[]{:S(2)}) copy-start(f32[128]{0:T(128)S(1)} %fusion.83) | copy-start | bytes 1540
  426.1 67.6 %copy-start.8 = (bf16[1,128,768]{2,1,0:T(8,128)(2,1)S(1)}, bf16[1,128,768]{2,1,0:T(8,128)(2,1)}, u32[]{:S(2)}) copy-start(bf16[1,128,768]{2,1,0:T(8,128)(2,1)} %param.24) | copy-start | bytes 589828
  429.4 69.7 %copy-start.3 = (f32[128,3072]{1,0:T(8,128)}, f32[128,3072]{1,0:T(8,128)S(1)}, u32[]{:S(2)}) copy-start(f32[128,3072]{1,0:T(8,128)S(1)} %convolution_add_fusion) | copy-start | bytes 4718596
  493.7 5.4 copy-start
  493.7 5.4 copy-start.22
  493.7 5.4 copy-start.29
  493.7 5.5 copy-start.34
  501.8 155.5 %copy-start.6 = (f32[128,768]{1,0:T(8,128)}, f32[128,768]{1,0:T(8,128)S(1)}, u32[]{:S(2)}) copy-start(f32[128,768]{1,0:T(8,128)S(1)} %get-tuple-element.677) | copy-start | bytes 1179652
  501.8 155.5 %copy-start.43 = (f32[128]{0:T(128)}, f32[128]{0:T(128)S(1)}, u32[]{:S(2)}) copy-start(f32[128]{0:T(128)S(1)} %negate_multiply_fusion.1) | copy-start | bytes 1540
  638.7 18.6 %copy-start.10 = (bf16[768,768]{1,0:T(8,128)(2,1)S(1)}, bf16[768,768]{1,0:T(8,128)(2,1)}, u32[]{:S(2)}) copy-start(bf16[768,768]{1,0:T(8,128)(2,1)} %all-gather.20.cloned.1.call-done) | copy-start | bytes 3538948
  795.2 542.0 %reduce-scatter.10.cloned.1.call-start = ((), (), s32[]{:S(2)}) async-start(), calls=%async_computation.14 | async-start | bytes 1769472 | tf_op jit(solution)/shard_map/reduce_scatter | solution.py:300
  797.8 606.0 %reduce-scatter.12.cloned.1.call-start = ((), (), s32[]{:S(2)}) async-start(), calls=%async_computation.15 | async-start | bytes 7077888 | tf_op jit(solution)/shard_map/reduce_scatter | solution.py:312
  801.7 668.4 %reduce-scatter.14.cloned.1.call-start = ((), (), s32[]{:S(2)}) async-start(), calls=%async_computation.16 | async-start | bytes 7077888 | tf_op jit(solution)/shard_map/reduce_scatter | solution.py:318
  806.9 504.1 %copy-start.20 = (f32[768]{0:T(1024)S(1)}, f32[768]{0:T(1024)}, u32[]{:S(2)}) copy-start(f32[768]{0:T(1024)} %copy-done.19) | copy-start | bytes 9220
  806.9 504.1 %copy-start.27 = (f32[768]{0:T(1024)S(1)}, f32[768]{0:T(1024)}, u32[]{:S(2)}) copy-start(f32[768]{0:T(1024)} %copy-done.26) | copy-start | bytes 9220
  806.9 504.1 %copy-start.32 = (f32[128]{0:T(128)S(1)}, f32[128]{0:T(128)}, u32[]{:S(2)}) copy-start(f32[128]{0:T(128)} %copy-done.31) | copy-start | bytes 1540
  806.9 717.3 %reduce-scatter.8.cloned.1.call-start = ((), (), s32[]{:S(2)}) async-start(), calls=%async_computation.13 | async-start | bytes 5308416 | tf_op jit(solution)/shard_map/reduce_scatter | solution.py:291
  808.4 506.2 %copy-start.17 = (bf16[128,768]{1,0:T(8,128)(2,1)}, bf16[128,768]{1,0:T(8,128)(2,1)S(1)}, u32[]{:S(2)}) copy-start(bf16[128,768]{1,0:T(8,128)(2,1)S(1)} %copy.100) | copy-start | bytes 589828
  1314.7 8.0 copy-start.57
  1325.2 144.9 %copy-start.15 = (f32[128,1536]{1,0:T(8,128)S(1)}, f32[128,1536]{1,0:T(8,128)}, u32[]{:S(2)}) copy-start(f32[128,1536]{1,0:T(8,128)} %reduce-scatter.6.cloned.1.call-done) | copy-start | bytes 2359300
  1329.3 144.5 %copy-start.54 = (f32[128]{0:T(128)S(1)}, f32[128]{0:T(128)}, u32[]{:S(2)}) copy-start(f32[128]{0:T(128)} %copy-done.53) | copy-start | bytes 1540
  1329.3 144.6 %copy-start.37 = (f32[128]{0:T(128)S(1)}, f32[128]{0:T(128)}, u32[]{:S(2)}) copy-start(f32[128]{0:T(128)} %copy-done.36) | copy-start | bytes 1540
  1329.3 144.9 %copy-start.45 = (f32[128]{0:T(128)S(1)}, f32[128]{0:T(128)}, u32[]{:S(2)}) copy-start(f32[128]{0:T(128)} %copy-done.43) | copy-start | bytes 1540
  1470.2 54.0 %copy-start.18 = (bf16[384,768]{1,0:T(8,128)(2,1)S(1)}, bf16[384,768]{1,0:T(8,128)(2,1)}, u32[]{:S(2)}) copy-start(bf16[384,768]{1,0:T(8,128)(2,1)} %reduce-scatter.10.cloned.1.call-done) | copy-start | bytes 1769476
  (22 other events, 59.6 us)
Sparse Core Ops, SparseCore 0:
  9.7 56.0 all-gather.15
  69.4 261.5 all-gather.17
  332.6 25.8 all-gather.19
  360.1 66.0 all-gather.21
  427.6 66.0 all-gather.23
  495.9 117.2 all-gather.25
  795.3 514.4 reduce-scatter.5
  1312.7 24.4 reduce-scatter.9
  1340.4 63.3 reduce-scatter.11
  1406.6 63.3 reduce-scatter.13
  1473.1 51.0 reduce-scatter.7
